TPU v7x, 256 devices: a whole 4x4x8 slice. The times are simulated.
256 devices in a mesh: sub: 32 (over x, z), col: 8 (over y, core).
Axes of the slice: x: 4, y: 4, z: 8, core: 2. Of those that a mesh axis runs over, the one named last changes fastest.
Arguments:
- trace_start: bfloat16 [32, 8, 1536, 128], P('sub', 'col'), may hold values from -6 to 6
- neumann_load: bfloat16 [32, 8, 1536, 128], P('sub', 'col'), may hold values from -6 to 6
- double_layer: bfloat16 [32, 8, 1536, 1536], P('sub', 'col'), may hold values from -0.15625 to 0.15625
- single_inverse: bfloat16 [32, 8, 1536, 1536], P('sub', 'col'), may hold values from -0.15625 to 0.15625
- interface_nodes: int32 [32, 8, 8, 128], P('sub', 'col'), may hold values from -1 to 1023, as said below
- node_mode: int32 [32, 8, 1536], P('sub', 'col'), may hold values from 0 to 63
- mode_weight: bfloat16 [32, 8, 1536], P('sub', 'col'), may hold values from 0.5 to 1.5
- coarse_inverse: bfloat16 [16384, 16384], P('sub', 'col'), may hold values from -0.005859375 to 0.005859375
Outputs:
- final_trace: bfloat16 [32, 8, 1536, 128], P('sub', 'col')
- final_residual: bfloat16 [32, 8, 1536, 128], P('sub', 'col')
Inputs may be any that keep to these rules, and one draw needn't show every extreme that they name: `interface_nodes`: entry k of block (s, d) is a boundary node of s, within nodes d * 128 to (d + 1) * 128 - 1, distinct within the block, and matches entry k of the neighbour's block for direction 7 - d; valid entries come first and the rest are -1; blocks toward outside the grid are all -1; blocks of directions 1, 3, 4, 6 have 128 / 2 to 128 valid entries, the others 1 to 16, and some block has 128.
All inputs are finite; a program needn't handle non-finite values.
Results may differ from a plain program's by a relative error of at most 0.019.
Values may be sent and summed in bfloat16 or wider, within the bound.
A program may use at most 64 MiB of HBM per device.

v0:
```python
import jax
import jax.numpy as jnp
from jax import lax
from jax.sharding import PartitionSpec as P

MODES = 64
ITERS = 3


DIRECTIONS = ((-1, -1), (-1, 0), (-1, 1), (0, -1), (0, 1), (1, -1), (1, 0), (1, 1))


def from_behind(value, axis, by):
    devices = lax.axis_size(axis)
    pairs = [(i, i + by) for i in range(devices) if 0 <= i + by < devices]
    return lax.ppermute(value, axis, pairs)


def deliver_single(outgoing):
    arrivals = []
    for toward in range(8):
        row_step, col_step = DIRECTIONS[toward]
        message = outgoing[7 - toward]
        if row_step != 0:
            message = from_behind(message, "sub", -row_step)
        if col_step != 0:
            message = from_behind(message, "col", -col_step)
        arrivals.append(message)
    return jnp.stack(arrivals)


def local(
    trace_start,
    neumann_load,
    double_layer,
    single_inverse,
    interface_nodes,
    node_mode,
    mode_weight,
    coarse_inverse,
):
    trace_now = trace_start[0, 0]
    load_block = neumann_load[0, 0].astype(jnp.float32)
    kernel = double_layer[0, 0]
    inverse = single_inverse[0, 0]
    node_count = kernel.shape[0]
    interface = interface_nodes[0, 0]
    slot_count = interface.shape[1]
    band_rows = 8 * slot_count
    local_index = interface - (jnp.arange(8, dtype=jnp.int32) * slot_count)[:, None]
    selector = (
        local_index[:, :, None] == jnp.arange(slot_count, dtype=jnp.int32)[None, None, :]
    ).astype(jnp.bfloat16)
    mode_basis = jnp.where(
        node_mode[0, 0][None, :] == jnp.arange(MODES, dtype=jnp.int32)[:, None],
        mode_weight[0, 0][None, :],
        jnp.zeros((), jnp.bfloat16),
    )
    rhs_count = trace_now.shape[1]
    residual = trace_now
    rest_zeros = jnp.zeros((node_count - band_rows, rhs_count), jnp.float32)
    for iteration in range(ITERS):
        mixed_trace = (
            0.5 * trace_now.astype(jnp.float32)
            + jnp.dot(kernel, trace_now, preferred_element_type=jnp.float32)
        ).astype(jnp.bfloat16)
        flux_now = jnp.dot(inverse, mixed_trace, preferred_element_type=jnp.float32).astype(
            jnp.bfloat16
        )
        banded = flux_now[:band_rows].reshape(8, slot_count, rhs_count)
        outgoing = jnp.einsum(
            "dpq,dqr->dpr", selector, banded, preferred_element_type=jnp.float32
        ).astype(jnp.bfloat16)
        received = deliver_single(outgoing)
        placed = jnp.einsum(
            "dpq,dpr->dqr", selector, received, preferred_element_type=jnp.float32
        ).reshape(band_rows, rhs_count)
        assembled = flux_now.astype(jnp.float32) + jnp.concatenate([placed, rest_zeros], axis=0)
        residual = (load_block - assembled).astype(jnp.bfloat16)
        residual = lax.optimization_barrier(residual)
        coarse_rhs = jnp.dot(mode_basis, residual, preferred_element_type=jnp.float32).astype(
            jnp.bfloat16
        )
        partial_value = jnp.dot(
            coarse_inverse,
            lax.all_gather(coarse_rhs, "sub", axis=0, tiled=True),
            preferred_element_type=jnp.float32,
        )
        coarse_out = lax.psum_scatter(
            partial_value.astype(jnp.bfloat16), "col", scatter_dimension=0, tiled=True
        )
        correction = lax.dot_general(
            mode_basis, coarse_out, (((0,), (0,)), ((), ())), preferred_element_type=jnp.float32
        )
        trace_now = (
            trace_now.astype(jnp.float32) + 0.25 * residual.astype(jnp.float32) + correction
        ).astype(jnp.bfloat16)
    return (trace_now[None, None], residual[None, None])


def solution(mesh):
    placed = (
        P("sub", "col", None, None),
        P("sub", "col", None, None),
        P("sub", "col", None, None),
        P("sub", "col", None, None),
        P("sub", "col", None, None),
        P("sub", "col", None),
        P("sub", "col", None),
        P("sub", "col"),
    )
    return jax.shard_map(
        local,
        mesh=mesh,
        in_specs=placed,
        out_specs=(P("sub", "col", None, None), P("sub", "col", None, None)),
        check_vma=False,
    )
```

profile of v0, /device:TPU:1, one launch (start us, length us, event | category | flops | bytes accessed | tf_op | source)
XLA Modules:
  0.0 429.0 jit_solution(12199868396667985276)
XLA Ops:
  8.6 7.1 %fusion.54 = bf16[1536,128]{0,1:T(8,128)(2,1)S(1)} fusion(bf16[1,1,1536,1536]{3,2,1,0:T(8,128)(2,1)} %param.11, bf16[1,1,1536,1536]{3,2,1,0:T(8,128)(2,1)} %param.10, bf16[1,1,1536,128]{3,2,1,0:T(8,128)(2,1)} %param.8, bf16[1,1,1536,128]{2,3,1,0:T(8,128)(2,1)S(1)} %copy.26), kind=kOutput, calls=%fused_computation.31 | convolution fusion | flops 1208942592 | bytes 10616832 | tf_op jit(solution)/shard_map/dot_general | solution.py:67
  16.3 5.0 %collective-permute-start = (bf16[128,128]{1,0:T(8,128)(2,1)S(1)}, bf16[128,128]{1,0:T(8,128)(2,1)}, u32[]{:S(2)}, u32[]{:S(2)}) collective-permute-start(bf16[128,128]{1,0:T(8,128)(2,1)S(1)} %get-tuple-element.29), channel_id=1, source_target_pairs={{0,8},{8,16},{16,24},{24,32},{32,40},{40,48},{48,56},{56,64},{64,7... | collective-permute-start | bytes 98312 | tf_op jit(solution)/shard_map/ppermute | solution.py:16
  21.7 4.6 %collective-permute-start.1 = (bf16[128,128]{1,0:T(8,128)(2,1)}, bf16[128,128]{1,0:T(8,128)(2,1)}, u32[]{:S(2)}, u32[]{:S(2)}) collective-permute-start(bf16[128,128]{1,0:T(8,128)(2,1)} %collective-permute-done), channel_id=1, source_target_pairs={{0,1},{1,2},{2,3},{3,4},{4,5},{5,6},{6,7},{8,9},{9,10},{10,11},{11... | collective-permute-start | bytes 98312 | tf_op jit(solution)/shard_map/ppermute | solution.py:16
  30.2 6.5 %collective-permute-start.3 = (bf16[128,128]{1,0:T(8,128)(2,1)S(1)}, bf16[128,128]{1,0:T(8,128)(2,1)}, u32[]{:S(2)}, u32[]{:S(2)}) collective-permute-start(bf16[128,128]{1,0:T(8,128)(2,1)S(1)} %get-tuple-element.27), channel_id=1, source_target_pairs={{0,8},{8,16},{16,24},{24,32},{32,40},{40,48},{48,56},{56,64},{64,7... | collective-permute-start | bytes 98312 | tf_op jit(solution)/shard_map/ppermute | solution.py:16
  38.7 3.0 collective-permute-start.2
  46.3 3.6 collective-permute-start.5
  51.9 3.6 collective-permute-start.8
  57.9 2.1 copy.49
  62.1 44.5 %all_gather.9 = bf16[2048,128]{1,0:T(8,128)(2,1)S(1)} all-gather(bf16[64,128]{1,0:T(8,128)(2,1)S(1)} %convolution_convert_fusion.8), channel_id=1, replica_groups=mesh['sub'=32,'col'=8] {'sub'}, dimensions={0}, use_global_device_ids=true | all-gather | bytes 540672 | tf_op jit(solution)/shard_map/all_gather | solution.py:86
  108.3 39.5 %reduce-scatter.10.cloned.1.call-done = bf16[64,128]{1,0:T(8,128)(2,1)} async-done(((bf16[512,128]{1,0:T(8,128)(2,1)}), bf16[64,128]{1,0:T(8,128)(2,1)}) %reduce-scatter.10.cloned.1.call-update) | async-done | bytes 16400
  149.2 6.9 %fusion.51 = bf16[1536,128]{0,1:T(8,128)(2,1)S(1)} fusion(bf16[1,1,1536,1536]{3,2,1,0:T(8,128)(2,1)} %param.11, bf16[1536,128]{0,1:T(8,128)(2,1)S(1)} %fusion.27, bf16[1,1,1536,1536]{3,2,1,0:T(8,128)(2,1)} %param.10), kind=kOutput, calls=%fused_computation.30 | convolution fusion | flops 1208942592 | bytes 10223616 | tf_op jit(solution)/shard_map/dot_general | solution.py:67
  158.3 2.9 collective-permute-start.12
  162.3 4.1 collective-permute-start.13
  170.2 5.8 %collective-permute-start.15 = (bf16[128,128]{1,0:T(8,128)(2,1)S(1)}, bf16[128,128]{1,0:T(8,128)(2,1)S(1)}, u32[]{:S(2)}, u32[]{:S(2)}) collective-permute-start(bf16[128,128]{1,0:T(8,128)(2,1)S(1)} %get-tuple-element.19), channel_id=1, source_target_pairs={{0,8},{8,16},{16,24},{24,32},{32,40},{40,48},{48,56},{56,64},{64,7... | collective-permute-start | bytes 98312 | tf_op jit(solution)/shard_map/ppermute | solution.py:16
  176.1 3.4 collective-permute-start.14
  179.5 3.9 collective-permute-start.18
  185.4 3.6 collective-permute-start.17
  191.0 3.6 collective-permute-start.20
  196.7 2.1 copy.51
  200.9 44.1 %all_gather.10 = bf16[2048,128]{1,0:T(8,128)(2,1)S(1)} all-gather(bf16[64,128]{1,0:T(8,128)(2,1)S(1)} %convolution_convert_fusion.7), channel_id=1, replica_groups=mesh['sub'=32,'col'=8] {'sub'}, dimensions={0}, use_global_device_ids=true | all-gather | bytes 540672 | tf_op jit(solution)/shard_map/all_gather | solution.py:86
  246.9 37.5 %reduce-scatter.12.cloned.1.call-done = bf16[64,128]{1,0:T(8,128)(2,1)} async-done(((bf16[512,128]{1,0:T(8,128)(2,1)}), bf16[64,128]{1,0:T(8,128)(2,1)}) %reduce-scatter.12.cloned.1.call-update) | async-done | bytes 16400
  285.7 6.9 %fusion.48 = bf16[1536,128]{0,1:T(8,128)(2,1)S(1)} fusion(bf16[1,1,1536,1536]{3,2,1,0:T(8,128)(2,1)} %param.11, bf16[1536,128]{0,1:T(8,128)(2,1)S(1)} %fusion.28, bf16[1,1,1536,1536]{3,2,1,0:T(8,128)(2,1)} %param.10), kind=kOutput, calls=%fused_computation.29 | convolution fusion | flops 1208942592 | bytes 10223616 | tf_op jit(solution)/shard_map/dot_general | solution.py:67
  294.9 3.0 collective-permute-start.24
  299.0 4.1 collective-permute-start.25
  306.9 5.8 %collective-permute-start.27 = (bf16[128,128]{1,0:T(8,128)(2,1)S(1)}, bf16[128,128]{1,0:T(8,128)(2,1)S(1)}, u32[]{:S(2)}, u32[]{:S(2)}) collective-permute-start(bf16[128,128]{1,0:T(8,128)(2,1)S(1)} %get-tuple-element.11), channel_id=1, source_target_pairs={{0,8},{8,16},{16,24},{24,32},{32,40},{40,48},{48,56},{56,64},{64,7... | collective-permute-start | bytes 98312 | tf_op jit(solution)/shard_map/ppermute | solution.py:16
  312.8 3.4 collective-permute-start.26
  316.2 3.9 collective-permute-start.30
  322.1 3.6 collective-permute-start.29
  327.7 3.6 collective-permute-start.32
  333.4 2.1 copy.53
  337.0 44.1 %all_gather.11 = bf16[2048,128]{1,0:T(8,128)(2,1)S(1)} all-gather(bf16[64,128]{1,0:T(8,128)(2,1)S(1)} %convolution_convert_fusion.6), channel_id=1, replica_groups=mesh['sub'=32,'col'=8] {'sub'}, dimensions={0}, use_global_device_ids=true | all-gather | bytes 540672 | tf_op jit(solution)/shard_map/all_gather | solution.py:86
  383.6 36.9 %reduce-scatter.14.cloned.1.call-done = bf16[64,128]{1,0:T(8,128)(2,1)} async-done(((bf16[512,128]{1,0:T(8,128)(2,1)}), bf16[64,128]{1,0:T(8,128)(2,1)}) %reduce-scatter.14.cloned.1.call-update) | async-done | bytes 16400
  (132 shorter events, 59.4 us)
Async XLA Ops:
  7.2 140.7 %reduce-scatter.10.cloned.1.call-start = ((), (), s32[]{:S(2)}) async-start(), calls=%async_computation.3 | async-start | bytes 147456
  21.7 17.0 %collective-permute-start.1 = (bf16[128,128]{1,0:T(8,128)(2,1)}, bf16[128,128]{1,0:T(8,128)(2,1)}, u32[]{:S(2)}, u32[]{:S(2)}) collective-permute-start(bf16[128,128]{1,0:T(8,128)(2,1)} %collective-permute-done), channel_id=1, source_target_pairs={{0,1},{1,2},{2,3},{3,4},{4,5},{5,6},{6,7},{8,9},{9,10},{10,11},{11... | collective-permute-start | bytes 98312 | tf_op jit(solution)/shard_map/ppermute | solution.py:16
  26.3 20.0 %collective-permute-start.10 = (bf16[128,128]{1,0:T(8,128)(2,1)S(1)}, bf16[128,128]{1,0:T(8,128)(2,1)}, u32[]{:S(2)}, u32[]{:S(2)}) collective-permute-start(bf16[128,128]{1,0:T(8,128)(2,1)S(1)} %get-tuple-element.22), channel_id=1, source_target_pairs={{8,0},{16,8},{24,16},{32,24},{40,32},{48,40},{56,48},{64,56},{72,6... | collective-permute-start | bytes 98312 | tf_op jit(solution)/shard_map/ppermute | solution.py:16
  27.6 29.3 %collective-permute-start.9 = (bf16[128,128]{1,0:T(8,128)(2,1)S(1)}, bf16[128,128]{1,0:T(8,128)(2,1)S(1)}, u32[]{:S(2)}, u32[]{:S(2)}) collective-permute-start(bf16[128,128]{1,0:T(8,128)(2,1)S(1)} %get-tuple-element.23), channel_id=1, source_target_pairs={{8,0},{16,8},{24,16},{32,24},{40,32},{48,40},{56,48},{64,56},{72,6... | collective-permute-start | bytes 98312 | tf_op jit(solution)/shard_map/ppermute | solution.py:16
  28.9 21.0 %collective-permute-start.7 = (bf16[128,128]{1,0:T(8,128)(2,1)S(1)}, bf16[128,128]{1,0:T(8,128)(2,1)}, u32[]{:S(2)}, u32[]{:S(2)}) collective-permute-start(bf16[128,128]{1,0:T(8,128)(2,1)S(1)} %get-tuple-element.24), channel_id=1, source_target_pairs={{8,0},{16,8},{24,16},{32,24},{40,32},{48,40},{56,48},{64,56},{72,6... | collective-permute-start | bytes 98312 | tf_op jit(solution)/shard_map/ppermute | solution.py:16
  30.2 12.2 %collective-permute-start.3 = (bf16[128,128]{1,0:T(8,128)(2,1)S(1)}, bf16[128,128]{1,0:T(8,128)(2,1)}, u32[]{:S(2)}, u32[]{:S(2)}) collective-permute-start(bf16[128,128]{1,0:T(8,128)(2,1)S(1)} %get-tuple-element.27), channel_id=1, source_target_pairs={{0,8},{8,16},{16,24},{24,32},{32,40},{40,48},{48,56},{56,64},{64,7... | collective-permute-start | bytes 98312 | tf_op jit(solution)/shard_map/ppermute | solution.py:16
  42.4 13.2 %collective-permute-start.6 = (bf16[128,128]{1,0:T(8,128)(2,1)S(1)}, bf16[128,128]{1,0:T(8,128)(2,1)S(1)}, u32[]{:S(2)}, u32[]{:S(2)}) collective-permute-start(bf16[128,128]{1,0:T(8,128)(2,1)S(1)} %get-tuple-element.25), channel_id=1, source_target_pairs={{1,0},{2,1},{3,2},{4,3},{5,4},{6,5},{7,6},{9,8},{10,9},{11,10},{12... | collective-permute-start | bytes 98312 | tf_op jit(solution)/shard_map/ppermute | solution.py:16
  44.3 7.5 %collective-permute-start.4 = (bf16[128,128]{1,0:T(8,128)(2,1)}, bf16[128,128]{1,0:T(8,128)(2,1)S(1)}, u32[]{:S(2)}, u32[]{:S(2)}) collective-permute-start(bf16[128,128]{1,0:T(8,128)(2,1)} %collective-permute-done.3), channel_id=1, source_target_pairs={{1,0},{2,1},{3,2},{4,3},{5,4},{6,5},{7,6},{9,8},{10,9},{11,10},{12... | collective-permute-start | bytes 98312 | tf_op jit(solution)/shard_map/ppermute | solution.py:16
  46.3 9.3 %collective-permute-start.5 = (bf16[128,128]{1,0:T(8,128)(2,1)S(1)}, bf16[128,128]{1,0:T(8,128)(2,1)S(1)}, u32[]{:S(2)}, u32[]{:S(2)}) collective-permute-start(bf16[128,128]{1,0:T(8,128)(2,1)S(1)} %get-tuple-element.26), channel_id=1, source_target_pairs={{0,1},{1,2},{2,3},{3,4},{4,5},{5,6},{6,7},{8,9},{9,10},{10,11},{11... | collective-permute-start | bytes 98312 | tf_op jit(solution)/shard_map/ppermute | solution.py:16
  50.0 6.9 %collective-permute-start.11 = (bf16[128,128]{1,0:T(8,128)(2,1)}, bf16[128,128]{1,0:T(8,128)(2,1)S(1)}, u32[]{:S(2)}, u32[]{:S(2)}) collective-permute-start(bf16[128,128]{1,0:T(8,128)(2,1)} %collective-permute-done.10), channel_id=1, source_target_pairs={{1,0},{2,1},{3,2},{4,3},{5,4},{6,5},{7,6},{9,8},{10,9},{11,10},{12... | collective-permute-start | bytes 98312 | tf_op jit(solution)/shard_map/ppermute | solution.py:16
  108.3 176.1 %reduce-scatter.12.cloned.1.call-start = ((), (), s32[]{:S(2)}) async-start(), calls=%async_computation.4 | async-start | bytes 147456
  162.3 13.8 %collective-permute-start.13 = (bf16[128,128]{1,0:T(8,128)(2,1)S(1)}, bf16[128,128]{1,0:T(8,128)(2,1)S(1)}, u32[]{:S(2)}, u32[]{:S(2)}) collective-permute-start(bf16[128,128]{1,0:T(8,128)(2,1)S(1)} %collective-permute-done.12), channel_id=1, source_target_pairs={{0,1},{1,2},{2,3},{3,4},{4,5},{5,6},{6,7},{8,9},{9,10},{10,11},{11... | collective-permute-start | bytes 98312 | tf_op jit(solution)/shard_map/ppermute | solution.py:16
  166.3 19.1 %collective-permute-start.22 = (bf16[128,128]{1,0:T(8,128)(2,1)S(1)}, bf16[128,128]{1,0:T(8,128)(2,1)S(1)}, u32[]{:S(2)}, u32[]{:S(2)}) collective-permute-start(bf16[128,128]{1,0:T(8,128)(2,1)S(1)} %get-tuple-element.14), channel_id=1, source_target_pairs={{8,0},{16,8},{24,16},{32,24},{40,32},{48,40},{56,48},{64,56},{72,6... | collective-permute-start | bytes 98312 | tf_op jit(solution)/shard_map/ppermute | solution.py:16
  167.6 28.0 %collective-permute-start.21 = (bf16[128,128]{1,0:T(8,128)(2,1)S(1)}, bf16[128,128]{1,0:T(8,128)(2,1)S(1)}, u32[]{:S(2)}, u32[]{:S(2)}) collective-permute-start(bf16[128,128]{1,0:T(8,128)(2,1)S(1)} %get-tuple-element.15), channel_id=1, source_target_pairs={{8,0},{16,8},{24,16},{32,24},{40,32},{48,40},{56,48},{64,56},{72,6... | collective-permute-start | bytes 98312 | tf_op jit(solution)/shard_map/ppermute | solution.py:16
  168.9 20.1 %collective-permute-start.19 = (bf16[128,128]{1,0:T(8,128)(2,1)S(1)}, bf16[128,128]{1,0:T(8,128)(2,1)S(1)}, u32[]{:S(2)}, u32[]{:S(2)}) collective-permute-start(bf16[128,128]{1,0:T(8,128)(2,1)S(1)} %get-tuple-element.16), channel_id=1, source_target_pairs={{8,0},{16,8},{24,16},{32,24},{40,32},{48,40},{56,48},{64,56},{72,6... | collective-permute-start | bytes 98312 | tf_op jit(solution)/shard_map/ppermute | solution.py:16
  170.2 9.2 %collective-permute-start.15 = (bf16[128,128]{1,0:T(8,128)(2,1)S(1)}, bf16[128,128]{1,0:T(8,128)(2,1)S(1)}, u32[]{:S(2)}, u32[]{:S(2)}) collective-permute-start(bf16[128,128]{1,0:T(8,128)(2,1)S(1)} %get-tuple-element.19), channel_id=1, source_target_pairs={{0,8},{8,16},{16,24},{24,32},{32,40},{40,48},{48,56},{56,64},{64,7... | collective-permute-start | bytes 98312 | tf_op jit(solution)/shard_map/ppermute | solution.py:16
  176.1 7.3 %collective-permute-start.14 = (bf16[128,128]{1,0:T(8,128)(2,1)S(1)}, bf16[128,128]{1,0:T(8,128)(2,1)S(1)}, u32[]{:S(2)}, u32[]{:S(2)}) collective-permute-start(bf16[128,128]{1,0:T(8,128)(2,1)S(1)} %get-tuple-element.20), channel_id=1, source_target_pairs={{0,8},{8,16},{16,24},{24,32},{32,40},{40,48},{48,56},{56,64},{64,7... | collective-permute-start | bytes 98312 | tf_op jit(solution)/shard_map/ppermute | solution.py:16
  179.5 15.2 %collective-permute-start.18 = (bf16[128,128]{1,0:T(8,128)(2,1)S(1)}, bf16[128,128]{1,0:T(8,128)(2,1)S(1)}, u32[]{:S(2)}, u32[]{:S(2)}) collective-permute-start(bf16[128,128]{1,0:T(8,128)(2,1)S(1)} %get-tuple-element.17), channel_id=1, source_target_pairs={{1,0},{2,1},{3,2},{4,3},{5,4},{6,5},{7,6},{9,8},{10,9},{11,10},{12... | collective-permute-start | bytes 98312 | tf_op jit(solution)/shard_map/ppermute | solution.py:16
  183.4 7.5 %collective-permute-start.16 = (bf16[128,128]{1,0:T(8,128)(2,1)S(1)}, bf16[128,128]{1,0:T(8,128)(2,1)S(1)}, u32[]{:S(2)}, u32[]{:S(2)}) collective-permute-start(bf16[128,128]{1,0:T(8,128)(2,1)S(1)} %collective-permute-done.15), channel_id=1, source_target_pairs={{1,0},{2,1},{3,2},{4,3},{5,4},{6,5},{7,6},{9,8},{10,9},{11,10},{12... | collective-permute-start | bytes 98312 | tf_op jit(solution)/shard_map/ppermute | solution.py:16
  185.4 9.3 %collective-permute-start.17 = (bf16[128,128]{1,0:T(8,128)(2,1)S(1)}, bf16[128,128]{1,0:T(8,128)(2,1)S(1)}, u32[]{:S(2)}, u32[]{:S(2)}) collective-permute-start(bf16[128,128]{1,0:T(8,128)(2,1)S(1)} %get-tuple-element.18), channel_id=1, source_target_pairs={{0,1},{1,2},{2,3},{3,4},{4,5},{5,6},{6,7},{8,9},{9,10},{10,11},{11... | collective-permute-start | bytes 98312 | tf_op jit(solution)/shard_map/ppermute | solution.py:16
  189.1 6.6 %collective-permute-start.23 = (bf16[128,128]{1,0:T(8,128)(2,1)S(1)}, bf16[128,128]{1,0:T(8,128)(2,1)S(1)}, u32[]{:S(2)}, u32[]{:S(2)}) collective-permute-start(bf16[128,128]{1,0:T(8,128)(2,1)S(1)} %collective-permute-done.22), channel_id=1, source_target_pairs={{1,0},{2,1},{3,2},{4,3},{5,4},{6,5},{7,6},{9,8},{10,9},{11,10},{12... | collective-permute-start | bytes 98312 | tf_op jit(solution)/shard_map/ppermute | solution.py:16
  246.6 173.9 %reduce-scatter.14.cloned.1.call-start = ((), (), s32[]{:S(2)}) async-start(), calls=%async_computation.5 | async-start | bytes 147456
  299.0 13.8 %collective-permute-start.25 = (bf16[128,128]{1,0:T(8,128)(2,1)S(1)}, bf16[128,128]{1,0:T(8,128)(2,1)S(1)}, u32[]{:S(2)}, u32[]{:S(2)}) collective-permute-start(bf16[128,128]{1,0:T(8,128)(2,1)S(1)} %collective-permute-done.24), channel_id=1, source_target_pairs={{0,1},{1,2},{2,3},{3,4},{4,5},{5,6},{6,7},{8,9},{9,10},{10,11},{11... | collective-permute-start | bytes 98312 | tf_op jit(solution)/shard_map/ppermute | solution.py:16
  303.0 19.1 %collective-permute-start.34 = (bf16[128,128]{1,0:T(8,128)(2,1)S(1)}, bf16[128,128]{1,0:T(8,128)(2,1)S(1)}, u32[]{:S(2)}, u32[]{:S(2)}) collective-permute-start(bf16[128,128]{1,0:T(8,128)(2,1)S(1)} %get-tuple-element.6), channel_id=1, source_target_pairs={{8,0},{16,8},{24,16},{32,24},{40,32},{48,40},{56,48},{64,56},{72,6... | collective-permute-start | bytes 98312 | tf_op jit(solution)/shard_map/ppermute | solution.py:16
  304.3 28.0 %collective-permute-start.33 = (bf16[128,128]{1,0:T(8,128)(2,1)S(1)}, bf16[128,128]{1,0:T(8,128)(2,1)S(1)}, u32[]{:S(2)}, u32[]{:S(2)}) collective-permute-start(bf16[128,128]{1,0:T(8,128)(2,1)S(1)} %get-tuple-element.7), channel_id=1, source_target_pairs={{8,0},{16,8},{24,16},{32,24},{40,32},{48,40},{56,48},{64,56},{72,6... | collective-permute-start | bytes 98312 | tf_op jit(solution)/shard_map/ppermute | solution.py:16
  305.6 20.1 %collective-permute-start.31 = (bf16[128,128]{1,0:T(8,128)(2,1)S(1)}, bf16[128,128]{1,0:T(8,128)(2,1)S(1)}, u32[]{:S(2)}, u32[]{:S(2)}) collective-permute-start(bf16[128,128]{1,0:T(8,128)(2,1)S(1)} %get-tuple-element.8), channel_id=1, source_target_pairs={{8,0},{16,8},{24,16},{32,24},{40,32},{48,40},{56,48},{64,56},{72,6... | collective-permute-start | bytes 98312 | tf_op jit(solution)/shard_map/ppermute | solution.py:16
  306.9 9.2 %collective-permute-start.27 = (bf16[128,128]{1,0:T(8,128)(2,1)S(1)}, bf16[128,128]{1,0:T(8,128)(2,1)S(1)}, u32[]{:S(2)}, u32[]{:S(2)}) collective-permute-start(bf16[128,128]{1,0:T(8,128)(2,1)S(1)} %get-tuple-element.11), channel_id=1, source_target_pairs={{0,8},{8,16},{16,24},{24,32},{32,40},{40,48},{48,56},{56,64},{64,7... | collective-permute-start | bytes 98312 | tf_op jit(solution)/shard_map/ppermute | solution.py:16
  312.8 7.3 %collective-permute-start.26 = (bf16[128,128]{1,0:T(8,128)(2,1)S(1)}, bf16[128,128]{1,0:T(8,128)(2,1)S(1)}, u32[]{:S(2)}, u32[]{:S(2)}) collective-permute-start(bf16[128,128]{1,0:T(8,128)(2,1)S(1)} %get-tuple-element.12), channel_id=1, source_target_pairs={{0,8},{8,16},{16,24},{24,32},{32,40},{40,48},{48,56},{56,64},{64,7... | collective-permute-start | bytes 98312 | tf_op jit(solution)/shard_map/ppermute | solution.py:16
  316.2 15.2 %collective-permute-start.30 = (bf16[128,128]{1,0:T(8,128)(2,1)S(1)}, bf16[128,128]{1,0:T(8,128)(2,1)S(1)}, u32[]{:S(2)}, u32[]{:S(2)}) collective-permute-start(bf16[128,128]{1,0:T(8,128)(2,1)S(1)} %get-tuple-element.9), channel_id=1, source_target_pairs={{1,0},{2,1},{3,2},{4,3},{5,4},{6,5},{7,6},{9,8},{10,9},{11,10},{12... | collective-permute-start | bytes 98312 | tf_op jit(solution)/shard_map/ppermute | solution.py:16
  320.1 7.5 %collective-permute-start.28 = (bf16[128,128]{1,0:T(8,128)(2,1)S(1)}, bf16[128,128]{1,0:T(8,128)(2,1)S(1)}, u32[]{:S(2)}, u32[]{:S(2)}) collective-permute-start(bf16[128,128]{1,0:T(8,128)(2,1)S(1)} %collective-permute-done.27), channel_id=1, source_target_pairs={{1,0},{2,1},{3,2},{4,3},{5,4},{6,5},{7,6},{9,8},{10,9},{11,10},{12... | collective-permute-start | bytes 98312 | tf_op jit(solution)/shard_map/ppermute | solution.py:16
  322.1 9.3 %collective-permute-start.29 = (bf16[128,128]{1,0:T(8,128)(2,1)S(1)}, bf16[128,128]{1,0:T(8,128)(2,1)S(1)}, u32[]{:S(2)}, u32[]{:S(2)}) collective-permute-start(bf16[128,128]{1,0:T(8,128)(2,1)S(1)} %get-tuple-element.10), channel_id=1, source_target_pairs={{0,1},{1,2},{2,3},{3,4},{4,5},{5,6},{6,7},{8,9},{9,10},{10,11},{11... | collective-permute-start | bytes 98312 | tf_op jit(solution)/shard_map/ppermute | solution.py:16
  325.7 6.6 %collective-permute-start.35 = (bf16[128,128]{1,0:T(8,128)(2,1)S(1)}, bf16[128,128]{1,0:T(8,128)(2,1)S(1)}, u32[]{:S(2)}, u32[]{:S(2)}) collective-permute-start(bf16[128,128]{1,0:T(8,128)(2,1)S(1)} %collective-permute-done.34), channel_id=1, source_target_pairs={{1,0},{2,1},{3,2},{4,3},{5,4},{6,5},{7,6},{9,8},{10,9},{11,10},{12... | collective-permute-start | bytes 98312 | tf_op jit(solution)/shard_map/ppermute | solution.py:16
  (13 other events, 211.7 us)
Sparse Core Ops, SparseCore 0:
  108.4 39.4 reduce-scatter.9
  246.8 37.5 reduce-scatter.11
  382.8 37.6 reduce-scatter.13
where the time goes:
time: 432 us; the launch traced here: 429 us
  blocking collectives  133 us (31%)
  waiting for transfers between devices  120 us (28%)
  starting transfers between devices  107 us (25%)
  matrix products  31.9 us (7%)
  local copies, waits for them, and re-layouts  19.3 us (4%)
  between operations  14.6 us (3%)
  other arithmetic  4.39 us (1%)
    all_gather x3, blocking collectives, local(): lax.all_gather(coarse_rhs, 'sub', axis=0, tiled=True)  133 us
    unnamed x6, waiting for transfers between devices  114 us
    ppermute x36, starting transfers between devices, from_behind(): return lax.ppermute(value, axis, pairs)  106 us
    dot_general x3, matrix products, local(): jnp.dot(inverse, mixed_trace, preferred_element_type=jnp.float32)  21 us
    unnamed x40, local copies, waits for them, and re-layouts  9.05 us
  transfers between devices with their start and end apart: 39, of which 9 were waited for; matrix products, arithmetic and copies ran while one was open for 1% of the time, Pallas kernels for 0%

commit v1 on v0

v1 whole, which is shorter than its diff:
```python
import functools

import jax
import jax.numpy as jnp
from jax import lax
from jax.experimental import pallas as pl
from jax.experimental.pallas import tpu as pltpu
from jax.sharding import PartitionSpec as P

MESH = pl.DeviceIdType.MESH
ITERS = 3
M = 1536
R = 128
MODES = 64
XS, ZS = 4, 8
SUB, COL = 32, 8
TILE = 256
TILES = M // TILE
FACES = (1, 3, 4, 6)
CORNERS = (0, 2, 5, 7)
STEPS = ((-1, -1), (-1, 0), (-1, 1), (0, -1), (0, 1), (1, -1), (1, 0), (1, 1))
CSLOTS = 16
ROWS_OUT = 5 * 128
REAL_OUT = 4 * 128 + 4 * CSLOTS
RELAY_UP = (0, 7, 2, 5)
RELAY_DOWN = (1, 6, 3, 4)
Z_ORDER = (4, 3, 5, 2, 6, 1, 7)
BF = jnp.bfloat16
F32 = jnp.float32


def dot(a, b):
    return jnp.dot(a, b, preferred_element_type=F32)


def kernel(
    trace_hbm, load_hbm, k_hbm, s_hbm, iface_ref, mode_ref, weight_ref, c_hbm,
    out_trace, out_resid,
    tv, lv, kv, sv, cv, x_ref, mx, flux, tr, rv, wb, basis,
    sel, sel_t, selc, selc_t, hb, wsel, bw, opart, rhsp, cb, pacc,
    obuf, ebuf, vbuf, pbuf, rbuf,
    in_sem, k_sem, s_sem, out_sem,
    ex_send, ex_recv, ag_send, zr, xr, dr, rs_send, rs_recv,
):
    a = lax.axis_index("sub")
    b = lax.axis_index("col")
    x = a // ZS
    z = a % ZS

    def wrap(i, n):
        return lax.rem(i + n, n)

    barrier = pltpu.get_barrier_semaphore()
    peers = [(wrap(a + STEPS[d][0], SUB), wrap(b + STEPS[d][1], COL)) for d in range(8)]
    greet = list(peers)
    greet += [(x * ZS + wrap(z + dz, ZS), b) for dz in range(1, ZS)]
    greet += [(wrap(x + dx, XS) * ZS + z, b) for dx in (1, -1)]
    greet += [(a, wrap(b + j, COL)) for j in range(1, COL)]
    for peer in greet:
        pl.semaphore_signal(barrier, inc=1, device_id=peer, device_id_type=MESH)

    def rows(i, n):
        return pl.ds(pl.multiple_of(i * n, n), n)

    cp_t = pltpu.make_async_copy(trace_hbm.at[0, 0], tv, in_sem.at[0])
    cp_l = pltpu.make_async_copy(load_hbm.at[0, 0], lv, in_sem.at[1])
    cp_c = pltpu.make_async_copy(c_hbm, cv, in_sem.at[2])

    def k_copy(i):
        return pltpu.make_async_copy(k_hbm.at[0, 0, rows(i, TILE)], kv.at[rows(i, TILE)], k_sem.at[i])

    def s_copy(i):
        return pltpu.make_async_copy(s_hbm.at[0, 0, rows(i, TILE)], sv.at[rows(i, TILE)], s_sem.at[i])

    cp_t.start()
    for i in range(TILES):
        k_copy(i).start()
    for i in range(TILES):
        s_copy(i).start()
    cp_l.start()
    cp_c.start()

    mode_row = mode_ref[0]
    weight_row = weight_ref[0].astype(F32)
    for j in range(M // 128):
        cols = slice(j * 128, (j + 1) * 128)
        part = jnp.where(
            lax.broadcasted_iota(jnp.int32, (128, 128), 0) == mode_row[:, cols],
            weight_row[:, cols],
            0.0,
        )
        basis[:, cols] = part.astype(BF)
        x_ref[cols, 128:] = part.T.astype(BF)

    slots_all = iface_ref[0, 0]
    node_iota = lax.broadcasted_iota(jnp.int32, (128, 128), 0)
    lane_iota = lax.broadcasted_iota(jnp.int32, (128, 128), 1)
    for f, d in enumerate(FACES):
        hot = jnp.where(node_iota == slots_all[d : d + 1] - 128 * d, 1.0, 0.0)
        sel_t[f] = hot.astype(BF)
        sel[f] = hot.T.astype(BF)
    for c, d in enumerate(CORNERS):
        moved = pltpu.roll(slots_all, CSLOTS * c, 1) if c else slots_all
        inside = (lane_iota >= CSLOTS * c) & (lane_iota < CSLOTS * (c + 1))
        hot = jnp.where((node_iota == moved[d : d + 1] - 128 * d) & inside, 1.0, 0.0)
        selc_t[c] = hot.astype(BF)
        selc[c] = hot.T.astype(BF)
    cb[...] = jnp.zeros_like(cb)
    for it in range(ITERS):
        ebuf[it, REAL_OUT:, :] = jnp.zeros((ROWS_OUT - REAL_OUT, R), BF)

    cp_t.wait()
    x_ref[:, :128] = tv[...]
    tr[...] = tv[...].astype(F32)

    def k_tile(i, width):
        span = rows(i, TILE)
        acc = dot(kv[span, :], x_ref[:, :width])
        mx[span, :width] = (acc + 0.5 * x_ref[span, :width].astype(F32)).astype(BF)

    def s_tile_first(i):
        span = rows(i, TILE)
        acc = dot(sv[span, :], mx[...])
        flux[span, :] = acc[:, :128]
        wb[span, :] = acc[:, 128:].astype(BF)

    def s_tile(i):
        span = rows(i, TILE)
        flux[span, :] = dot(sv[span, :], mx[:, :128])

    def band(d):
        return slice(128 * d, 128 * (d + 1))

    def select_from(source):
        pieces = [dot(sel[f], source(band(d))) for f, d in enumerate(FACES)]
        corner = dot(selc[0], source(band(CORNERS[0])))
        for c in range(1, 4):
            corner += dot(selc[c], source(band(CORNERS[c])))
        return pieces + [corner]

    @pl.loop(0, TILES)
    def _(i):
        k_copy(i).wait()
        k_tile(i, 256)

    @pl.loop(0, 4)
    def _(i):
        s_copy(i).wait()
        s_tile_first(i)

    def rhs_of_flux():
        rhsp[...] = dot(basis[...], (lv[...].astype(F32) - flux[...]).astype(BF))

    def send_outgoing(it):
        copies = []
        for d in CORNERS:
            c = CORNERS.index(d)
            there = 512 + CSLOTS * (3 - c)
            here = 512 + CSLOTS * c
            copies.append((peers[d], slice(here, here + CSLOTS), slice(there, there + CSLOTS)))
        for f, d in enumerate(FACES):
            copies.append((peers[d], band(f), band(3 - f)))
        for peer, here, there in copies:
            pltpu.make_async_remote_copy(
                src_ref=obuf.at[it, here], dst_ref=ebuf.at[it, there],
                send_sem=ex_send.at[it], recv_sem=ex_recv.at[it],
                device_id=peer, device_id_type=MESH,
            ).start()

    def wait_bytes(ref, sem):
        pltpu.make_async_copy(ref, ref, sem).wait()

    def slot(ax, az):
        return pl.ds(pl.multiple_of((ax * ZS + az) * MODES, MODES), MODES)

    def send_block(it, where, sem, peer):
        pltpu.make_async_remote_copy(
            src_ref=vbuf.at[it, where], dst_ref=vbuf.at[it, where],
            send_sem=ag_send.at[it], recv_sem=sem, device_id=peer, device_id_type=MESH,
        ).start()

    up = (wrap(x + 1, XS) * ZS + z, b)
    down = (wrap(x - 1, XS) * ZS + z, b)

    def send_z(it):
        own = slot(x, z)
        for dz in Z_ORDER:
            send_block(it, own, zr.at[it, dz - 1], (x * ZS + wrap(z + dz, ZS), b))

    def send_x(it, dz):
        where = slot(x, wrap(z - dz, ZS))
        k_up = RELAY_UP.index(dz) if dz in RELAY_UP else 4
        k_down = RELAY_DOWN.index(dz) if dz in RELAY_DOWN else 4
        send_block(it, where, xr.at[it, 0, k_up], up)
        send_block(it, where, xr.at[it, 1, k_down], down)

    def got_z(it, dz):
        wait_bytes(vbuf.at[it, slot(x, wrap(z - dz, ZS))], zr.at[it, dz - 1])
        send_x(it, dz)

    def relay(it, k):
        where = slot(wrap(x - 1, XS), wrap(z - RELAY_UP[k], ZS))
        wait_bytes(vbuf.at[it, where], xr.at[it, 0, k])
        send_block(it, where, dr.at[it], up)
        where = slot(wrap(x + 1, XS), wrap(z - RELAY_DOWN[k], ZS))
        wait_bytes(vbuf.at[it, where], xr.at[it, 1, k])
        send_block(it, where, dr.at[it], down)

    def coarse_row(it, dx, first):
        span = pl.ds(pl.multiple_of(wrap(x + dx, XS) * (ZS * MODES), ZS * MODES), ZS * MODES)
        part = dot(cv[:, span], vbuf[it, span, :])
        if first:
            pacc[...] = part
        else:
            pacc[...] += part

    def residual_bands(it, group):
        for d in group:
            span = band(d)
            assembled = flux[span, :]
            if d < 8:
                if d in FACES:
                    f = FACES.index(d)
                    assembled += dot(sel_t[f], ebuf[it, band(f), :])
                else:
                    assembled += dot(selc_t[CORNERS.index(d)], ebuf[it, 512:, :])
            resid = (lv[span, :].astype(F32) - assembled).astype(BF)
            rv[span, :] = resid
            moved = tr[span, :] + 0.25 * resid.astype(F32)
            tr[span, :] = moved
            x_ref[span, :128] = moved.astype(BF)

    for it in range(ITERS):
        last = it == ITERS - 1
        if it == 0:
            source = lambda span: flux[span, :].astype(BF)
            for j, piece in enumerate(select_from(source)):
                obuf[it, band(j), :] = piece.astype(BF)
            pl.semaphore_wait(barrier, len(greet))
            send_outgoing(it)

            @pl.loop(4, TILES)
            def _(i):
                s_copy(i).wait()
                s_tile_first(i)

            cp_l.wait()
            cp_c.wait()
            for j, piece in enumerate(select_from(lambda span: wb[span, :])):
                wsel[band(j), :] = piece.astype(BF)
            bw[...] = dot(basis[...], wb[...]).astype(BF)
            for f, d in enumerate(FACES):
                hb[:, band(f)] = dot(basis[:, band(d)], sel_t[f]).astype(BF)
            corner = dot(basis[:, band(CORNERS[0])], selc_t[0])
            for c in range(1, 4):
                corner += dot(basis[:, band(CORNERS[c])], selc_t[c])
            hb[:, 512:] = corner.astype(BF)
            rhs_of_flux()
        else:
            obuf[it] = (opart[...] + dot(wsel[...], cb[...])).astype(BF)
            send_outgoing(it)
            rhsp[...] -= dot(bw[...], cb[...])
            flux[...] += dot(wb[...], cb[...])
            tr[...] += dot(x_ref[:, 128:], cb[...])

        wait_bytes(ebuf.at[it, :REAL_OUT], ex_recv.at[it])
        rhs = rhsp[...] - dot(hb[...], ebuf[it])
        vbuf[it, slot(x, z), :] = rhs[:MODES].astype(BF)
        send_z(it)
        send_x(it, 0)

        jobs = [
            functools.partial(residual_bands, it, range(0, 6)),
            functools.partial(residual_bands, it, range(6, 12)),
        ]
        if not last:
            jobs += [functools.partial(k_tile, i, 128) for i in range(TILES)]
            jobs += [functools.partial(s_tile, i) for i in range(TILES)]

            def finish():
                source = lambda span: flux[span, :].astype(BF)
                for j, piece in enumerate(select_from(source)):
                    opart[band(j), :] = piece
                rhs_of_flux()

            jobs.append(finish)

        def work(n):
            for _ in range(min(n, len(jobs))):
                jobs.pop(0)()

        work(3)
        got_z(it, 1)
        got_z(it, 7)
        relay(it, 0)
        work(2)
        got_z(it, 2)
        got_z(it, 6)
        work(2)
        relay(it, 1)
        got_z(it, 3)
        got_z(it, 5)
        work(1)
        got_z(it, 4)
        coarse_row(it, 0, True)
        relay(it, 2)
        work(2)
        relay(it, 3)
        for side in range(2):
            wait_bytes(vbuf.at[it, : 4 * MODES], xr.at[it, side, 4])
        coarse_row(it, 1, False)
        coarse_row(it, -1, False)
        wait_bytes(vbuf.at[it, : 8 * MODES], dr.at[it])
        coarse_row(it, 2, False)

        pbuf[it] = pacc[...].astype(BF)
        for j in Z_ORDER:
            to = wrap(b + j, COL)
            pltpu.make_async_remote_copy(
                src_ref=pbuf.at[it, rows(to, MODES)], dst_ref=rbuf.at[it, rows(j, MODES)],
                send_sem=rs_send.at[it], recv_sem=rs_recv.at[it],
                device_id=(a, to), device_id_type=MESH,
            ).start()
        if last:
            cp_r = pltpu.make_async_copy(rv, out_resid, out_sem.at[0])
            cp_r.start()
        work(len(jobs))
        wait_bytes(rbuf.at[it, MODES:], rs_recv.at[it])
        total = pacc[rows(b, MODES), :]
        for j in range(1, COL):
            total += rbuf[it, j * MODES : (j + 1) * MODES, :].astype(F32)
        cb[:MODES, :] = total.astype(BF)

    tv[...] = (tr[...] + dot(x_ref[:, 128:], cb[...])).astype(BF)
    cp_o = pltpu.make_async_copy(tv, out_trace, out_sem.at[1])
    cp_o.start()
    for it in range(ITERS):
        wait_bytes(obuf.at[it, :REAL_OUT], ex_send.at[it])
        wait_bytes(vbuf.at[it, : (SUB - 1) * MODES], ag_send.at[it])
        wait_bytes(pbuf.at[it, MODES:], rs_send.at[it])
    cp_r.wait()
    cp_o.wait()


def local(trace_start, neumann_load, double_layer, single_inverse, interface_nodes, node_mode, mode_weight, coarse_inverse):
    hbm = pl.BlockSpec(memory_space=pl.ANY)
    vmem = pl.BlockSpec(memory_space=pltpu.VMEM)
    square = lambda: pltpu.VMEM((M, M), BF)
    tall = lambda kind: pltpu.VMEM((M, R), kind)
    dma = pltpu.SemaphoreType.DMA
    trace, resid = pl.pallas_call(
        kernel,
        out_shape=(jax.ShapeDtypeStruct((M, R), BF), jax.ShapeDtypeStruct((M, R), BF)),
        in_specs=[hbm, hbm, hbm, hbm, vmem, vmem, vmem, hbm],
        out_specs=(hbm, hbm),
        scratch_shapes=[
            tall(BF), tall(BF), square(), square(), pltpu.VMEM((512, 2048), BF),
            pltpu.VMEM((M, 256), BF), pltpu.VMEM((M, 256), BF), tall(F32), tall(F32), tall(BF), tall(BF),
            pltpu.VMEM((128, M), BF),
            pltpu.VMEM((4, 128, 128), BF), pltpu.VMEM((4, 128, 128), BF),
            pltpu.VMEM((4, 128, 128), BF), pltpu.VMEM((4, 128, 128), BF),
            pltpu.VMEM((128, ROWS_OUT), BF), pltpu.VMEM((ROWS_OUT, 128), BF), pltpu.VMEM((128, 128), BF),
            pltpu.VMEM((ROWS_OUT, R), F32), pltpu.VMEM((128, R), F32), pltpu.VMEM((128, R), BF),
            pltpu.VMEM((512, R), F32),
            pltpu.VMEM((ITERS, ROWS_OUT, R), BF), pltpu.VMEM((ITERS, ROWS_OUT, R), BF),
            pltpu.VMEM((ITERS, SUB * MODES, R), BF),
            pltpu.VMEM((ITERS, COL * MODES, R), BF), pltpu.VMEM((ITERS, COL * MODES, R), BF),
            dma((3,)), dma((TILES,)), dma((TILES,)), dma((2,)),
            dma((ITERS,)), dma((ITERS,)), dma((ITERS,)), dma((ITERS, 7)), dma((ITERS, 2, 5)), dma((ITERS,)),
            dma((ITERS,)), dma((ITERS,)),
        ],
        compiler_params=pltpu.CompilerParams(collective_id=0, has_side_effects=True),
    )(trace_start, neumann_load, double_layer, single_inverse, interface_nodes, node_mode, mode_weight, coarse_inverse)
    return trace[None, None], resid[None, None]


def solution(mesh):
    four = P("sub", "col", None, None)
    three = P("sub", "col", None)
    return jax.shard_map(
        local,
        mesh=mesh,
        in_specs=(four, four, four, four, four, three, three, P("sub", "col")),
        out_specs=(four, four),
        check_vma=False,
    )
```

time: 432 us -> 99.4 us (0.23)
  blocking collectives: 133 us -> 0 us
  waiting for transfers between devices: 120 us -> 0 us
  starting transfers between devices: 107 us -> 0 us
  Pallas kernels: 0 us -> 95 us
  matrix products: 31.9 us -> 0 us
  local copies, waits for them, and re-layouts: 19.3 us -> 3.53 us
  between operations: 14.6 us -> 0.64 us
  other arithmetic: 4.39 us -> 0 us
    all_gather x3 -> x0, blocking collectives: 133 us -> none  [local(): lax.all_gather(coarse_rhs, 'sub', axis=0, tiled=True)]
    unnamed x6 -> x0, waiting for transfers between devices: 114 us -> none
    ppermute x36 -> x0, starting transfers between devices: 106 us -> none  [from_behind(): return lax.ppermute(value, axis, pairs)]
    pallas_call x0 -> x1, Pallas kernels: none -> 95 us  [local(): pl.pallas_call(kernel, out_shape=(jax.ShapeDtypeStruct((M, R), BF), jax.S...]
    dot_general x18 -> x0, matrix products: 31.9 us -> none  [the longest x3 21 us: local(): jnp.dot(inverse, mixed_trace, preferred_element_type=jnp.float32)]
    reshape x6 -> x0, local copies, waits for them, and re-layouts: 8.57 us -> none  [the longest x3 6.17 us: local(): placed = jnp.einsum('dpq,dpr->dqr', selector, received, preferred_element...]
    ppermute x36 -> x0, waiting for transfers between devices: 5.62 us -> none  [from_behind(): return lax.ppermute(value, axis, pairs)]
    unnamed x40 -> x2, local copies, waits for them, and re-layouts: 9.05 us -> 3.53 us
  transfers between devices with their start and end apart: 39 -> 0, of which waited for: 9 -> 0; matrix products, arithmetic and copies ran while one was open for 1% -> 0% of each run, Pallas kernels for 0% -> 0%
where the time goes in v1:
time: 99.4 us; the launch traced here: 99.2 us
  Pallas kernels  95 us (96%)
  local copies, waits for them, and re-layouts  3.53 us (4%)
    pallas_call x1, Pallas kernels, local(): pl.pallas_call(kernel, out_shape=(jax.ShapeDtypeStruct((M, R), BF), jax.S...  95 us
    unnamed x2, local copies, waits for them, and re-layouts  3.53 us

profile of v1, /device:TPU:1, one launch (start us, length us, event | category | flops | bytes accessed | tf_op | source)
XLA Modules:
  0.0 99.2 jit_solution(14591894896217523372)
XLA Ops:
  0.6 95.0 %shard_map.95 = (bf16[1536,128]{1,0:T(8,128)(2,1)}, bf16[1536,128]{1,0:T(8,128)(2,1)}) custom-call(bf16[1,1,1536,128]{3,2,1,0:T(8,128)(2,1)} %trace_hbm.1, bf16[1,1,1536,128]{3,2,1,0:T(8,128)(2,1)} %load_hbm.1, bf16[1,1,1536,1536]{3,2,1,0:T(8,128)(2,1)} %k_hbm.1, bf16[1,1,1536,1536]{3,2,1,0:T(8,128)(2,1)} %s_hbm.1, s32[1,1,8,128]{3,2,1,0:T(8,128)} %iface_ref.1, ...), custom_call_target="tpu_custom_call" | custom-call | tf_op jit(solution)/shard_map/pallas_call | solution.py:351
  95.6 1.8 %copy.12 = bf16[1,1,1536,128]{3,2,1,0:T(8,128)(2,1)} copy(bf16[1,1,1536,128]{3,2,1,0:T(8,128)(2,1)} %bitcast.3) | data formatting | bytes 786432
  97.4 1.8 %copy.13 = bf16[1,1,1536,128]{3,2,1,0:T(8,128)(2,1)} copy(bf16[1,1,1536,128]{3,2,1,0:T(8,128)(2,1)} %bitcast.2) | data formatting | bytes 786432

commit v2 on v1

--- a/solution.py
+++ b/solution.py
@@ -22,8 +22,6 @@
 CSLOTS = 16
 ROWS_OUT = 5 * 128
 REAL_OUT = 4 * 128 + 4 * CSLOTS
-RELAY_UP = (0, 7, 2, 5)
-RELAY_DOWN = (1, 6, 3, 4)
 Z_ORDER = (4, 3, 5, 2, 6, 1, 7)
 BF = jnp.bfloat16
 F32 = jnp.float32
@@ -36,11 +34,11 @@
 def kernel(
     trace_hbm, load_hbm, k_hbm, s_hbm, iface_ref, mode_ref, weight_ref, c_hbm,
     out_trace, out_resid,
-    tv, lv, kv, sv, cv, x_ref, mx, flux, tr, rv, wb, basis,
+    tv, lv, kv, sv, cv, x_ref, mx, flux, tr, wb, basis,
     sel, sel_t, selc, selc_t, hb, wsel, bw, opart, rhsp, cb, pacc,
     obuf, ebuf, vbuf, pbuf, rbuf,
-    in_sem, k_sem, s_sem, out_sem,
-    ex_send, ex_recv, ag_send, zr, xr, dr, rs_send, rs_recv,
+    in_sem, k_sem, s_sem,
+    ex_send, ex_recv, ag_send, zr, xr, x_own, zf, rs_send, rs_recv,
 ):
     a = lax.axis_index("sub")
     b = lax.axis_index("col")
@@ -50,15 +48,11 @@
     def wrap(i, n):
         return lax.rem(i + n, n)
 
-    barrier = pltpu.get_barrier_semaphore()
     peers = [(wrap(a + STEPS[d][0], SUB), wrap(b + STEPS[d][1], COL)) for d in range(8)]
     greet = list(peers)
     greet += [(x * ZS + wrap(z + dz, ZS), b) for dz in range(1, ZS)]
-    greet += [(wrap(x + dx, XS) * ZS + z, b) for dx in (1, -1)]
+    greet += [(wrap(x + dx, XS) * ZS + z, b) for dx in range(1, XS)]
     greet += [(a, wrap(b + j, COL)) for j in range(1, COL)]
-    for peer in greet:
-        pl.semaphore_signal(barrier, inc=1, device_id=peer, device_id_type=MESH)
-
     def rows(i, n):
         return pl.ds(pl.multiple_of(i * n, n), n)
 
@@ -75,22 +69,9 @@
     cp_t.start()
     for i in range(TILES):
         k_copy(i).start()
-    for i in range(TILES):
-        s_copy(i).start()
-    cp_l.start()
-    cp_c.start()
-
-    mode_row = mode_ref[0]
-    weight_row = weight_ref[0].astype(F32)
-    for j in range(M // 128):
-        cols = slice(j * 128, (j + 1) * 128)
-        part = jnp.where(
-            lax.broadcasted_iota(jnp.int32, (128, 128), 0) == mode_row[:, cols],
-            weight_row[:, cols],
-            0.0,
-        )
-        basis[:, cols] = part.astype(BF)
-        x_ref[cols, 128:] = part.T.astype(BF)
+    barrier = pltpu.get_barrier_semaphore()
+    for peer in greet:
+        pl.semaphore_signal(barrier, inc=1, device_id=peer, device_id_type=MESH)
 
     slots_all = iface_ref[0, 0]
     node_iota = lax.broadcasted_iota(jnp.int32, (128, 128), 0)
@@ -113,8 +94,8 @@
     x_ref[:, :128] = tv[...]
     tr[...] = tv[...].astype(F32)
 
-    def k_tile(i, width):
-        span = rows(i, TILE)
+    def k_tile(i, width, tile=TILE):
+        span = rows(i, tile)
         acc = dot(kv[span, :], x_ref[:, :width])
         mx[span, :width] = (acc + 0.5 * x_ref[span, :width].astype(F32)).astype(BF)
 
@@ -124,8 +105,8 @@
         flux[span, :] = acc[:, :128]
         wb[span, :] = acc[:, 128:].astype(BF)
 
-    def s_tile(i):
-        span = rows(i, TILE)
+    def s_tile(i, tile=TILE):
+        span = rows(i, tile)
         flux[span, :] = dot(sv[span, :], mx[:, :128])
 
     def band(d):
@@ -138,15 +119,36 @@
             corner += dot(selc[c], source(band(CORNERS[c])))
         return pieces + [corner]
 
-    @pl.loop(0, TILES)
+    def build_basis():
+        mode_row = mode_ref[0]
+        weight_row = weight_ref[0].astype(F32)
+        for j in range(M // 128):
+            cols = slice(j * 128, (j + 1) * 128)
+            part = jnp.where(
+                lax.broadcasted_iota(jnp.int32, (128, 128), 0) == mode_row[:, cols],
+                weight_row[:, cols],
+                0.0,
+            )
+            basis[:, cols] = part.astype(BF)
+            x_ref[cols, 128:] = part.T.astype(BF)
+
+    for i in range(TILES):
+        s_copy(i).start()
+    cp_l.start()
+    cp_c.start()
+    for i in range(TILES):
+        k_copy(i).wait()
+
+    @pl.loop(0, M // 512)
     def _(i):
-        k_copy(i).wait()
-        k_tile(i, 256)
-
-    @pl.loop(0, 4)
+        k_tile(i, 128, 512)
+
+    for i in range(4):
+        s_copy(i).wait()
+
+    @pl.loop(0, 2)
     def _(i):
-        s_copy(i).wait()
-        s_tile_first(i)
+        s_tile(i, 512)
 
     def rhs_of_flux():
         rhsp[...] = dot(basis[...], (lv[...].astype(F32) - flux[...]).astype(BF))
@@ -179,8 +181,6 @@
             send_sem=ag_send.at[it], recv_sem=sem, device_id=peer, device_id_type=MESH,
         ).start()
 
-    up = (wrap(x + 1, XS) * ZS + z, b)
-    down = (wrap(x - 1, XS) * ZS + z, b)
 
     def send_z(it):
         own = slot(x, z)
@@ -189,22 +189,25 @@
 
     def send_x(it, dz):
         where = slot(x, wrap(z - dz, ZS))
-        k_up = RELAY_UP.index(dz) if dz in RELAY_UP else 4
-        k_down = RELAY_DOWN.index(dz) if dz in RELAY_DOWN else 4
-        send_block(it, where, xr.at[it, 0, k_up], up)
-        send_block(it, where, xr.at[it, 1, k_down], down)
+        sems = x_own if dz == 0 else xr
+        for dx in (2, 1, 3):
+            send_block(it, where, sems.at[it, dx - 1], (wrap(x + dx, XS) * ZS + z, b))
 
     def got_z(it, dz):
         wait_bytes(vbuf.at[it, slot(x, wrap(z - dz, ZS))], zr.at[it, dz - 1])
-        send_x(it, dz)
-
-    def relay(it, k):
-        where = slot(wrap(x - 1, XS), wrap(z - RELAY_UP[k], ZS))
-        wait_bytes(vbuf.at[it, where], xr.at[it, 0, k])
-        send_block(it, where, dr.at[it], up)
-        where = slot(wrap(x + 1, XS), wrap(z - RELAY_DOWN[k], ZS))
-        wait_bytes(vbuf.at[it, where], xr.at[it, 1, k])
-        send_block(it, where, dr.at[it], down)
+        if dz not in (1, ZS - 1):
+            send_x(it, dz)
+
+    def got_own_x(it, dx):
+        where = slot(wrap(x - dx, XS), z)
+        wait_bytes(vbuf.at[it, where], x_own.at[it, dx - 1])
+        for dz in (1, ZS - 1):
+            send_block(it, where, zf.at[it, dx - 1], (x * ZS + wrap(z + dz, ZS), b))
+
+    def got_x(it, dx):
+        wait_bytes(vbuf.at[it, : 2 * MODES], zf.at[it, dx - 1])
+        wait_bytes(vbuf.at[it, : (ZS - 3) * MODES], xr.at[it, dx - 1])
+        coarse_row(it, -dx, False)
 
     def coarse_row(it, dx, first):
         span = pl.ds(pl.multiple_of(wrap(x + dx, XS) * (ZS * MODES), ZS * MODES), ZS * MODES)
@@ -225,7 +228,8 @@
                 else:
                     assembled += dot(selc_t[CORNERS.index(d)], ebuf[it, 512:, :])
             resid = (lv[span, :].astype(F32) - assembled).astype(BF)
-            rv[span, :] = resid
+            if it == ITERS - 1:
+                out_resid[span, :] = resid
             moved = tr[span, :] + 0.25 * resid.astype(F32)
             tr[span, :] = moved
             x_ref[span, :128] = moved.astype(BF)
@@ -239,22 +243,18 @@
             pl.semaphore_wait(barrier, len(greet))
             send_outgoing(it)
 
-            @pl.loop(4, TILES)
-            def _(i):
+            for i in range(4, TILES):
                 s_copy(i).wait()
-                s_tile_first(i)
-
-            cp_l.wait()
-            cp_c.wait()
-            for j, piece in enumerate(select_from(lambda span: wb[span, :])):
-                wsel[band(j), :] = piece.astype(BF)
-            bw[...] = dot(basis[...], wb[...]).astype(BF)
+            s_tile(2, 512)
+
+            build_basis()
             for f, d in enumerate(FACES):
                 hb[:, band(f)] = dot(basis[:, band(d)], sel_t[f]).astype(BF)
             corner = dot(basis[:, band(CORNERS[0])], selc_t[0])
             for c in range(1, 4):
                 corner += dot(basis[:, band(CORNERS[c])], selc_t[c])
             hb[:, 512:] = corner.astype(BF)
+            cp_l.wait()
             rhs_of_flux()
         else:
             obuf[it] = (opart[...] + dot(wsel[...], cb[...])).astype(BF)
@@ -266,18 +266,23 @@
         wait_bytes(ebuf.at[it, :REAL_OUT], ex_recv.at[it])
         rhs = rhsp[...] - dot(hb[...], ebuf[it])
         vbuf[it, slot(x, z), :] = rhs[:MODES].astype(BF)
+        send_x(it, 0)
         send_z(it)
-        send_x(it, 0)
 
         jobs = [
             functools.partial(residual_bands, it, range(0, 6)),
             functools.partial(residual_bands, it, range(6, 12)),
         ]
         if not last:
-            jobs += [functools.partial(k_tile, i, 128) for i in range(TILES)]
-            jobs += [functools.partial(s_tile, i) for i in range(TILES)]
-
-            def finish():
+            width, product = (256, s_tile_first) if it == 0 else (128, s_tile)
+            jobs += [functools.partial(k_tile, i, width) for i in range(TILES)]
+            jobs += [functools.partial(product, i) for i in range(TILES)]
+
+            def finish(it=it):
+                if it == 0:
+                    for j, piece in enumerate(select_from(lambda span: wb[span, :])):
+                        wsel[band(j), :] = piece.astype(BF)
+                    bw[...] = dot(basis[...], wb[...]).astype(BF)
                 source = lambda span: flux[span, :].astype(BF)
                 for j, piece in enumerate(select_from(source)):
                     opart[band(j), :] = piece
@@ -289,29 +294,24 @@
             for _ in range(min(n, len(jobs))):
                 jobs.pop(0)()
 
-        work(3)
+        work(6)
+        got_own_x(it, 1)
+        got_own_x(it, 3)
+        got_own_x(it, 2)
+        got_z(it, 2)
+        got_z(it, 6)
+        got_z(it, 3)
+        got_z(it, 5)
+        got_z(it, 4)
+        work(5)
+        if it == 0:
+            cp_c.wait()
         got_z(it, 1)
         got_z(it, 7)
-        relay(it, 0)
-        work(2)
-        got_z(it, 2)
-        got_z(it, 6)
-        work(2)
-        relay(it, 1)
-        got_z(it, 3)
-        got_z(it, 5)
-        work(1)
-        got_z(it, 4)
         coarse_row(it, 0, True)
-        relay(it, 2)
-        work(2)
-        relay(it, 3)
-        for side in range(2):
-            wait_bytes(vbuf.at[it, : 4 * MODES], xr.at[it, side, 4])
-        coarse_row(it, 1, False)
-        coarse_row(it, -1, False)
-        wait_bytes(vbuf.at[it, : 8 * MODES], dr.at[it])
-        coarse_row(it, 2, False)
+        got_x(it, 1)
+        got_x(it, 3)
+        got_x(it, 2)
 
         pbuf[it] = pacc[...].astype(BF)
         for j in Z_ORDER:
@@ -321,9 +321,6 @@
                 send_sem=rs_send.at[it], recv_sem=rs_recv.at[it],
                 device_id=(a, to), device_id_type=MESH,
             ).start()
-        if last:
-            cp_r = pltpu.make_async_copy(rv, out_resid, out_sem.at[0])
-            cp_r.start()
         work(len(jobs))
         wait_bytes(rbuf.at[it, MODES:], rs_recv.at[it])
         total = pacc[rows(b, MODES), :]
@@ -331,15 +328,20 @@
             total += rbuf[it, j * MODES : (j + 1) * MODES, :].astype(F32)
         cb[:MODES, :] = total.astype(BF)
 
-    tv[...] = (tr[...] + dot(x_ref[:, 128:], cb[...])).astype(BF)
-    cp_o = pltpu.make_async_copy(tv, out_trace, out_sem.at[1])
-    cp_o.start()
+    out_trace[...] = (tr[...] + dot(x_ref[:, 128:], cb[...])).astype(BF)
     for it in range(ITERS):
         wait_bytes(obuf.at[it, :REAL_OUT], ex_send.at[it])
         wait_bytes(vbuf.at[it, : (SUB - 1) * MODES], ag_send.at[it])
         wait_bytes(pbuf.at[it, MODES:], rs_send.at[it])
-    cp_r.wait()
-    cp_o.wait()
+
+
+def store_kernel(trace_ref, resid_ref, out_trace, out_resid, sem):
+    first = pltpu.make_async_copy(trace_ref, out_trace.at[0, 0], sem.at[0])
+    second = pltpu.make_async_copy(resid_ref, out_resid.at[0, 0], sem.at[1])
+    first.start()
+    second.start()
+    first.wait()
+    second.wait()
 
 
 def local(trace_start, neumann_load, double_layer, single_inverse, interface_nodes, node_mode, mode_weight, coarse_inverse):
@@ -350,12 +352,12 @@
     dma = pltpu.SemaphoreType.DMA
     trace, resid = pl.pallas_call(
         kernel,
-        out_shape=(jax.ShapeDtypeStruct((M, R), BF), jax.ShapeDtypeStruct((M, R), BF)),
+        out_shape=(pltpu.VMEM((M, R), BF), pltpu.VMEM((M, R), BF)),
         in_specs=[hbm, hbm, hbm, hbm, vmem, vmem, vmem, hbm],
-        out_specs=(hbm, hbm),
+        out_specs=(vmem, vmem),
         scratch_shapes=[
             tall(BF), tall(BF), square(), square(), pltpu.VMEM((512, 2048), BF),
-            pltpu.VMEM((M, 256), BF), pltpu.VMEM((M, 256), BF), tall(F32), tall(F32), tall(BF), tall(BF),
+            pltpu.VMEM((M, 256), BF), pltpu.VMEM((M, 256), BF), tall(F32), tall(F32), tall(BF),
             pltpu.VMEM((128, M), BF),
             pltpu.VMEM((4, 128, 128), BF), pltpu.VMEM((4, 128, 128), BF),
             pltpu.VMEM((4, 128, 128), BF), pltpu.VMEM((4, 128, 128), BF),
@@ -365,13 +367,20 @@
             pltpu.VMEM((ITERS, ROWS_OUT, R), BF), pltpu.VMEM((ITERS, ROWS_OUT, R), BF),
             pltpu.VMEM((ITERS, SUB * MODES, R), BF),
             pltpu.VMEM((ITERS, COL * MODES, R), BF), pltpu.VMEM((ITERS, COL * MODES, R), BF),
-            dma((3,)), dma((TILES,)), dma((TILES,)), dma((2,)),
-            dma((ITERS,)), dma((ITERS,)), dma((ITERS,)), dma((ITERS, 7)), dma((ITERS, 2, 5)), dma((ITERS,)),
+            dma((3,)), dma((TILES,)), dma((TILES,)),
+            dma((ITERS,)), dma((ITERS,)), dma((ITERS,)), dma((ITERS, 7)), dma((ITERS, 3)), dma((ITERS, 3)), dma((ITERS, 3)),
             dma((ITERS,)), dma((ITERS,)),
         ],
         compiler_params=pltpu.CompilerParams(collective_id=0, has_side_effects=True),
     )(trace_start, neumann_load, double_layer, single_inverse, interface_nodes, node_mode, mode_weight, coarse_inverse)
-    return trace[None, None], resid[None, None]
+    return pl.pallas_call(
+        store_kernel,
+        out_shape=(jax.ShapeDtypeStruct((1, 1, M, R), BF), jax.ShapeDtypeStruct((1, 1, M, R), BF)),
+        in_specs=[hbm, hbm],
+        out_specs=(hbm, hbm),
+        scratch_shapes=[dma((2,))],
+        compiler_params=pltpu.CompilerParams(vmem_limit_bytes=1 << 20),
+    )(trace, resid)
 
 
 def solution(mesh):

time: 99.4 us -> 73.2 us (0.74)
  Pallas kernels: 95 us -> 72.4 us
  local copies, waits for them, and re-layouts: 3.53 us -> 0 us
    pallas_call x1 -> x2, Pallas kernels: 95 us -> 72.4 us  [the longest x1 71.5 us: local(): pl.pallas_call(kernel, out_shape=(pltpu.VMEM((M, R), BF), pltpu.VMEM((M,...]
    unnamed x2 -> x0, local copies, waits for them, and re-layouts: 3.53 us -> none
where the time goes in v2:
time: 73.2 us; the launch traced here: 73 us
  Pallas kernels  72.4 us (99%)
    pallas_call x1, Pallas kernels, local(): pl.pallas_call(kernel, out_shape=(pltpu.VMEM((M, R), BF), pltpu.VMEM((M,...  71.5 us

profile of v2, /device:TPU:1, one launch (start us, length us, event | category | flops | bytes accessed | tf_op | source)
XLA Modules:
  0.0 73.0 jit_solution(7866899900180791735)
XLA Ops:
  0.6 71.5 %shard_map.95 = (bf16[1536,128]{1,0:T(8,128)(2,1)S(1)}, bf16[1536,128]{1,0:T(8,128)(2,1)S(1)}) custom-call(bf16[1,1,1536,128]{3,2,1,0:T(8,128)(2,1)} %trace_hbm.1, bf16[1,1,1536,128]{3,2,1,0:T(8,128)(2,1)} %load_hbm.1, bf16[1,1,1536,1536]{3,2,1,0:T(8,128)(2,1)} %k_hbm.1, bf16[1,1,1536,1536]{3,2,1,0:T(8,128)(2,1)} %s_hbm.1, s32[1,1,8,128]{3,2,1,0:T(8,128)} %iface_ref.1, ...), custom_call_target="tpu_custom_call" | custom-call | tf_op jit(solution)/shard_map/pallas_call | solution.py:353
  72.1 0.9 %shard_map.96 = (bf16[1,1,1536,128]{3,2,1,0:T(8,128)(2,1)}, bf16[1,1,1536,128]{3,2,1,0:T(8,128)(2,1)}) custom-call(bf16[1536,128]{1,0:T(8,128)(2,1)S(1)} %get-tuple-element.4.trace_ref, bf16[1536,128]{1,0:T(8,128)(2,1)S(1)} %get-tuple-element.5.resid_ref), custom_call_target="tpu_custom_call" | custom-call | tf_op jit(solution)/shard_map/pallas_call | solution.py:376

commit v3 on v2

--- a/solution.py
+++ b/solution.py
@@ -23,6 +23,8 @@
 ROWS_OUT = 5 * 128
 REAL_OUT = 4 * 128 + 4 * CSLOTS
 Z_ORDER = (4, 3, 5, 2, 6, 1, 7)
+X_ORDER = (1, 3, 2)
+X_FIRST = {1: (1, 7), 2: (3, 5, 2, 6, 1, 7), 3: (1, 7)}
 BF = jnp.bfloat16
 F32 = jnp.float32
 
@@ -37,13 +39,15 @@
     tv, lv, kv, sv, cv, x_ref, mx, flux, tr, wb, basis,
     sel, sel_t, selc, selc_t, hb, wsel, bw, opart, rhsp, cb, pacc,
     obuf, ebuf, vbuf, pbuf, rbuf,
-    in_sem, k_sem, s_sem,
-    ex_send, ex_recv, ag_send, zr, xr, x_own, zf, rs_send, rs_recv,
+    in_sem,
+    ex_send, ex_recv, ag_send, zr, xr, x_own, rs_send, rs_recv,
 ):
     a = lax.axis_index("sub")
     b = lax.axis_index("col")
     x = a // ZS
     z = a % ZS
+    y = b // 2
+    core = b % 2
 
     def wrap(i, n):
         return lax.rem(i + n, n)
@@ -60,15 +64,18 @@
     cp_l = pltpu.make_async_copy(load_hbm.at[0, 0], lv, in_sem.at[1])
     cp_c = pltpu.make_async_copy(c_hbm, cv, in_sem.at[2])
 
+    def load_rows(hbm, vmem, first, last, sem):
+        span = pl.ds(first, last - first)
+        return pltpu.make_async_copy(hbm.at[0, 0, span], vmem.at[span], sem)
+
     def k_copy(i):
-        return pltpu.make_async_copy(k_hbm.at[0, 0, rows(i, TILE)], kv.at[rows(i, TILE)], k_sem.at[i])
-
-    def s_copy(i):
-        return pltpu.make_async_copy(s_hbm.at[0, 0, rows(i, TILE)], sv.at[rows(i, TILE)], s_sem.at[i])
-
+        span = rows(i, 512)
+        return pltpu.make_async_copy(k_hbm.at[0, 0, span], kv.at[span], in_sem.at[3 + i])
+
+    s_copies = [load_rows(s_hbm, sv, 0, 1024, in_sem.at[6]), load_rows(s_hbm, sv, 1024, M, in_sem.at[7])]
     cp_t.start()
-    for i in range(TILES):
-        k_copy(i).start()
+    k_copy(0).start()
+
     barrier = pltpu.get_barrier_semaphore()
     for peer in greet:
         pl.semaphore_signal(barrier, inc=1, device_id=peer, device_id_type=MESH)
@@ -80,6 +87,7 @@
         hot = jnp.where(node_iota == slots_all[d : d + 1] - 128 * d, 1.0, 0.0)
         sel_t[f] = hot.astype(BF)
         sel[f] = hot.T.astype(BF)
+    k_copy(1).start()
     for c, d in enumerate(CORNERS):
         moved = pltpu.roll(slots_all, CSLOTS * c, 1) if c else slots_all
         inside = (lane_iota >= CSLOTS * c) & (lane_iota < CSLOTS * (c + 1))
@@ -90,6 +98,11 @@
     for it in range(ITERS):
         ebuf[it, REAL_OUT:, :] = jnp.zeros((ROWS_OUT - REAL_OUT, R), BF)
 
+    k_copy(2).start()
+    for copy in s_copies:
+        copy.start()
+    cp_l.start()
+    cp_c.start()
     cp_t.wait()
     x_ref[:, :128] = tv[...]
     tr[...] = tv[...].astype(F32)
@@ -132,19 +145,12 @@
             basis[:, cols] = part.astype(BF)
             x_ref[cols, 128:] = part.T.astype(BF)
 
-    for i in range(TILES):
-        s_copy(i).start()
-    cp_l.start()
-    cp_c.start()
-    for i in range(TILES):
+    @pl.loop(0, 3)
+    def _(i):
         k_copy(i).wait()
-
-    @pl.loop(0, M // 512)
-    def _(i):
         k_tile(i, 128, 512)
 
-    for i in range(4):
-        s_copy(i).wait()
+    s_copies[0].wait()
 
     @pl.loop(0, 2)
     def _(i):
@@ -190,23 +196,26 @@
     def send_x(it, dz):
         where = slot(x, wrap(z - dz, ZS))
         sems = x_own if dz == 0 else xr
-        for dx in (2, 1, 3):
+        for dx in X_ORDER:
+            if dz in X_FIRST[dx]:
+                continue
             send_block(it, where, sems.at[it, dx - 1], (wrap(x + dx, XS) * ZS + z, b))
 
     def got_z(it, dz):
         wait_bytes(vbuf.at[it, slot(x, wrap(z - dz, ZS))], zr.at[it, dz - 1])
-        if dz not in (1, ZS - 1):
-            send_x(it, dz)
+        send_x(it, dz)
 
     def got_own_x(it, dx):
         where = slot(wrap(x - dx, XS), z)
         wait_bytes(vbuf.at[it, where], x_own.at[it, dx - 1])
-        for dz in (1, ZS - 1):
-            send_block(it, where, zf.at[it, dx - 1], (x * ZS + wrap(z + dz, ZS), b))
+        for dz in X_FIRST[dx]:
+            send_block(it, where, xr.at[it, dx - 1], (x * ZS + wrap(z + dz, ZS), b))
+
+    def wait_x(it, dx):
+        wait_bytes(vbuf.at[it, : (ZS - 1) * MODES], xr.at[it, dx - 1])
 
     def got_x(it, dx):
-        wait_bytes(vbuf.at[it, : 2 * MODES], zf.at[it, dx - 1])
-        wait_bytes(vbuf.at[it, : (ZS - 3) * MODES], xr.at[it, dx - 1])
+        wait_x(it, dx)
         coarse_row(it, -dx, False)
 
     def coarse_row(it, dx, first):
@@ -243,8 +252,7 @@
             pl.semaphore_wait(barrier, len(greet))
             send_outgoing(it)
 
-            for i in range(4, TILES):
-                s_copy(i).wait()
+            s_copies[1].wait()
             s_tile(2, 512)
 
             build_basis()
@@ -314,10 +322,10 @@
         got_x(it, 2)
 
         pbuf[it] = pacc[...].astype(BF)
-        for j in Z_ORDER:
-            to = wrap(b + j, COL)
+        for dy, dc in ((2, 0), (2, 1), (1, 0), (3, 0), (1, 1), (3, 1), (0, 1)):
+            to = 2 * wrap(y + dy, 4) + wrap(core + dc, 2)
             pltpu.make_async_remote_copy(
-                src_ref=pbuf.at[it, rows(to, MODES)], dst_ref=rbuf.at[it, rows(j, MODES)],
+                src_ref=pbuf.at[it, rows(to, MODES)], dst_ref=rbuf.at[it, rows(2 * dy + dc, MODES)],
                 send_sem=rs_send.at[it], recv_sem=rs_recv.at[it],
                 device_id=(a, to), device_id_type=MESH,
             ).start()
@@ -367,8 +375,8 @@
             pltpu.VMEM((ITERS, ROWS_OUT, R), BF), pltpu.VMEM((ITERS, ROWS_OUT, R), BF),
             pltpu.VMEM((ITERS, SUB * MODES, R), BF),
             pltpu.VMEM((ITERS, COL * MODES, R), BF), pltpu.VMEM((ITERS, COL * MODES, R), BF),
-            dma((3,)), dma((TILES,)), dma((TILES,)),
-            dma((ITERS,)), dma((ITERS,)), dma((ITERS,)), dma((ITERS, 7)), dma((ITERS, 3)), dma((ITERS, 3)), dma((ITERS, 3)),
+            dma((8,)),
+            dma((ITERS,)), dma((ITERS,)), dma((ITERS,)), dma((ITERS, 7)), dma((ITERS, 3)), dma((ITERS, 3)),
             dma((ITERS,)), dma((ITERS,)),
         ],
         compiler_params=pltpu.CompilerParams(collective_id=0, has_side_effects=True),

time: 73.2 us -> 69.5 us (0.949)
  Pallas kernels: 72.4 us -> 68.7 us
    pallas_call x1, Pallas kernels: 71.5 us -> 67.8 us  [local(): pl.pallas_call(kernel, out_shape=(pltpu.VMEM((M, R), BF), pltpu.VMEM((M,...]
where the time goes in v3:
time: 69.5 us; the launch traced here: 69.4 us
  Pallas kernels  68.7 us (99%)
    pallas_call x1, Pallas kernels, local(): pl.pallas_call(kernel, out_shape=(pltpu.VMEM((M, R), BF), pltpu.VMEM((M,...  67.8 us

profile of v3, /device:TPU:1, one launch (start us, length us, event | category | flops | bytes accessed | tf_op | source)
XLA Modules:
  0.0 69.4 jit_solution(2578356192508392384)
XLA Ops:
  0.6 67.8 %shard_map.95 = (bf16[1536,128]{1,0:T(8,128)(2,1)S(1)}, bf16[1536,128]{1,0:T(8,128)(2,1)S(1)}) custom-call(bf16[1,1,1536,128]{3,2,1,0:T(8,128)(2,1)} %trace_hbm.1, bf16[1,1,1536,128]{3,2,1,0:T(8,128)(2,1)} %load_hbm.1, bf16[1,1,1536,1536]{3,2,1,0:T(8,128)(2,1)} %k_hbm.1, bf16[1,1,1536,1536]{3,2,1,0:T(8,128)(2,1)} %s_hbm.1, s32[1,1,8,128]{3,2,1,0:T(8,128)} %iface_ref.1, ...), custom_call_target="tpu_custom_call" | custom-call | tf_op jit(solution)/shard_map/pallas_call | solution.py:361
  68.5 0.9 %shard_map.96 = (bf16[1,1,1536,128]{3,2,1,0:T(8,128)(2,1)}, bf16[1,1,1536,128]{3,2,1,0:T(8,128)(2,1)}) custom-call(bf16[1536,128]{1,0:T(8,128)(2,1)S(1)} %get-tuple-element.4.trace_ref, bf16[1536,128]{1,0:T(8,128)(2,1)S(1)} %get-tuple-element.5.resid_ref), custom_call_target="tpu_custom_call" | custom-call | tf_op jit(solution)/shard_map/pallas_call | solution.py:384

commit v4 on v3

--- a/solution.py
+++ b/solution.py
@@ -64,15 +64,14 @@
     cp_l = pltpu.make_async_copy(load_hbm.at[0, 0], lv, in_sem.at[1])
     cp_c = pltpu.make_async_copy(c_hbm, cv, in_sem.at[2])
 
-    def load_rows(hbm, vmem, first, last, sem):
-        span = pl.ds(first, last - first)
-        return pltpu.make_async_copy(hbm.at[0, 0, span], vmem.at[span], sem)
-
     def k_copy(i):
         span = rows(i, 512)
         return pltpu.make_async_copy(k_hbm.at[0, 0, span], kv.at[span], in_sem.at[3 + i])
 
-    s_copies = [load_rows(s_hbm, sv, 0, 1024, in_sem.at[6]), load_rows(s_hbm, sv, 1024, M, in_sem.at[7])]
+    def s_copy(i):
+        span = rows(i, 512)
+        return pltpu.make_async_copy(s_hbm.at[0, 0, span], sv.at[span], in_sem.at[6 + i])
+
     cp_t.start()
     k_copy(0).start()
 
@@ -99,10 +98,8 @@
         ebuf[it, REAL_OUT:, :] = jnp.zeros((ROWS_OUT - REAL_OUT, R), BF)
 
     k_copy(2).start()
-    for copy in s_copies:
-        copy.start()
-    cp_l.start()
-    cp_c.start()
+    for i in range(3):
+        s_copy(i).start()
     cp_t.wait()
     x_ref[:, :128] = tv[...]
     tr[...] = tv[...].astype(F32)
@@ -150,11 +147,13 @@
         k_copy(i).wait()
         k_tile(i, 128, 512)
 
-    s_copies[0].wait()
-
     @pl.loop(0, 2)
     def _(i):
+        s_copy(i).wait()
         s_tile(i, 512)
+
+    cp_l.start()
+    cp_c.start()
 
     def rhs_of_flux():
         rhsp[...] = dot(basis[...], (lv[...].astype(F32) - flux[...]).astype(BF))
@@ -252,7 +251,7 @@
             pl.semaphore_wait(barrier, len(greet))
             send_outgoing(it)
 
-            s_copies[1].wait()
+            s_copy(2).wait()
             s_tile(2, 512)
 
             build_basis()
@@ -302,7 +301,7 @@
             for _ in range(min(n, len(jobs))):
                 jobs.pop(0)()
 
-        work(6)
+        work(4)
         got_own_x(it, 1)
         got_own_x(it, 3)
         got_own_x(it, 2)
@@ -311,7 +310,7 @@
         got_z(it, 3)
         got_z(it, 5)
         got_z(it, 4)
-        work(5)
+        work(4 if it else 2)
         if it == 0:
             cp_c.wait()
         got_z(it, 1)
@@ -375,7 +374,7 @@
             pltpu.VMEM((ITERS, ROWS_OUT, R), BF), pltpu.VMEM((ITERS, ROWS_OUT, R), BF),
             pltpu.VMEM((ITERS, SUB * MODES, R), BF),
             pltpu.VMEM((ITERS, COL * MODES, R), BF), pltpu.VMEM((ITERS, COL * MODES, R), BF),
-            dma((8,)),
+            dma((9,)),
             dma((ITERS,)), dma((ITERS,)), dma((ITERS,)), dma((ITERS, 7)), dma((ITERS, 3)), dma((ITERS, 3)),
             dma((ITERS,)), dma((ITERS,)),
         ],

time: 69.5 us -> 69.7 us (level)
  no operation moved by 1% of the time
where the time goes in v4:
time: 69.7 us; the launch traced here: 69.6 us
  Pallas kernels  69 us (99%)
    pallas_call x1, Pallas kernels, local(): pl.pallas_call(kernel, out_shape=(pltpu.VMEM((M, R), BF), pltpu.VMEM((M,...  68.1 us

profile of v4, /device:TPU:1, one launch (start us, length us, event | category | flops | bytes accessed | tf_op | source)
XLA Modules:
  0.0 69.6 jit_solution(16123419927829678880)
XLA Ops:
  0.6 68.1 %shard_map.95 = (bf16[1536,128]{1,0:T(8,128)(2,1)S(1)}, bf16[1536,128]{1,0:T(8,128)(2,1)S(1)}) custom-call(bf16[1,1,1536,128]{3,2,1,0:T(8,128)(2,1)} %trace_hbm.1, bf16[1,1,1536,128]{3,2,1,0:T(8,128)(2,1)} %load_hbm.1, bf16[1,1,1536,1536]{3,2,1,0:T(8,128)(2,1)} %k_hbm.1, bf16[1,1,1536,1536]{3,2,1,0:T(8,128)(2,1)} %s_hbm.1, s32[1,1,8,128]{3,2,1,0:T(8,128)} %iface_ref.1, ...), custom_call_target="tpu_custom_call" | custom-call | tf_op jit(solution)/shard_map/pallas_call | solution.py:360
  68.7 0.9 %shard_map.96 = (bf16[1,1,1536,128]{3,2,1,0:T(8,128)(2,1)}, bf16[1,1,1536,128]{3,2,1,0:T(8,128)(2,1)}) custom-call(bf16[1536,128]{1,0:T(8,128)(2,1)S(1)} %get-tuple-element.4.trace_ref, bf16[1536,128]{1,0:T(8,128)(2,1)S(1)} %get-tuple-element.5.resid_ref), custom_call_target="tpu_custom_call" | custom-call | tf_op jit(solution)/shard_map/pallas_call | solution.py:383
